TPU v7x, 128 devices: a whole 4x4x4 slice. The times are simulated.
128 devices in a mesh: req: 8 (over x, core), tok: 16 (over z, y).
Axes of the slice: x: 4, y: 4, z: 4, core: 2. Of those that a mesh axis runs over, the one named last changes fastest.
Arguments:
- hidden: bfloat16 [8, 2048, 2048], P('req', 'tok'), may hold values from -4 to 4
- queries: bfloat16 [8, 2048, 3072], P('req', 'tok'), may hold values from -18 to 18
- fresh_latent: bfloat16 [8, 2048, 576], P('req', 'tok'), may hold values from -8 to 8
- latent_cache: bfloat16 [8, 16, 128, 576], P('req', 'tok'), may hold values from -8 to 8
- page_table: int32 [8, 16], P('req'), may hold values from 0 to 15, each once within a row
- cache_lengths: int32 [8], P('req'), may hold values from 2 to 2048, as said below
- routes: int32 [8, 2048, 6], P('req', 'tok'), may hold values from 0 to 63, all different within a row; in each aligned block of 128 rows (0 to 127, 128 to 255, ..., all dimensions but the last counted through in order) at most 14 rows name the same one
- route_gates: float32 [8, 2048, 6], P('req', 'tok'), may hold values from 0.05 to 0.45
- kv_up: bfloat16 [512, 4096], replicated, may hold values from -0.25 to 0.25
- out_proj: bfloat16 [2048, 2048], replicated, may hold values from -0.125 to 0.125
- latent_gain: float32 [512], replicated, may hold values from 0.1 to 1.9
- norm_gain: float32 [2048], replicated, may hold values from 0.1 to 1.9
- expert_in: bfloat16 [128, 2048, 1408], P(('req', 'tok')), may hold values from -0.125 to 0.125
- expert_out: bfloat16 [128, 704, 2048], P(('req', 'tok')), may hold values from -0.15625 to 0.15625
Outputs:
- layer_out: bfloat16 [8, 2048, 2048], P('req', 'tok')
- new_latent: bfloat16 [8, 2048, 576], P('req', 'tok')
Inputs may be any that keep to these rules, and one draw needn't show every extreme that they name: `page_table`: each request's row names every pool page once. `cache_lengths`: some request has exactly 2048 cached tokens. `routes`: the 6 experts of a token differ; among the rows of one device no expert is named more than 14 times, and that bound is reached.
All inputs are finite; a program needn't handle non-finite values.
Results may differ from a plain program's by a relative error of at most 0.013.
Values may be sent and summed in bfloat16 or wider, within the bound.
A program may use at most 192 MiB of HBM per device.

v0:
```python
import math

import jax
import jax.numpy as jnp
from jax import lax
from jax.sharding import PartitionSpec as P

H = 16
NOPE = 128
VD = 128
EXPERTS = 64
CAP = 14


epsilon = 1e-06
theta_base = 10000.0
floor_score = -1e30


def rotary(values, angles):
    half_width = values.shape[-1] // 2
    front_part = values[..., :half_width]
    back_part = values[..., half_width:]
    cosine = jnp.cos(angles)
    sine_part = jnp.sin(angles)
    return jnp.concatenate(
        [front_part * cosine - back_part * sine_part, back_part * cosine + front_part * sine_part],
        axis=-1,
    )


def rms_scale(values, gain):
    return values * lax.rsqrt(jnp.mean(values * values, axis=-1, keepdims=True) + epsilon) * gain


def local(
    hidden,
    queries,
    fresh_latent,
    latent_cache,
    page_table,
    cache_lengths,
    routes,
    route_gates,
    kv_up,
    out_proj,
    latent_gain,
    norm_gain,
    expert_in,
    expert_out,
):
    row_count = hidden.shape[1]
    model_width = hidden.shape[2]
    latent_width = latent_gain.shape[0]
    entry_width = fresh_latent.shape[2]
    rotary_width = entry_width - latent_width
    score_scale = 1.0 / math.sqrt(NOPE + rotary_width)
    length = cache_lengths[0]
    first_row = lax.axis_index("tok") * row_count
    positions = length + first_row + jnp.arange(row_count, dtype=jnp.int32)
    frequency = theta_base ** (
        -jnp.arange(rotary_width // 2, dtype=jnp.float32) * 2.0 / rotary_width
    )
    angles = positions.astype(jnp.float32)[:, None] * frequency[None, :]
    raw_latent = fresh_latent[0].astype(jnp.float32)
    latent = rms_scale(raw_latent[:, :latent_width], latent_gain).astype(jnp.bfloat16)
    key_rotated = rotary(raw_latent[:, latent_width:], angles).astype(jnp.bfloat16)
    query_rows = queries[0].reshape(row_count, H, NOPE + rotary_width)
    query_rotated = rotary(query_rows[:, :, NOPE:].astype(jnp.float32), angles[:, None, :]).astype(
        jnp.bfloat16
    )
    weights = kv_up.reshape(latent_width, H, NOPE + VD)
    query_latent = jnp.einsum(
        "thn,lhn->thl",
        query_rows[:, :, :NOPE],
        weights[:, :, :NOPE],
        preferred_element_type=jnp.float32,
    ).astype(jnp.bfloat16)

    def attend(carry, keys_latent, keys_rotated, key_positions, key_valid):
        highest, totals, accumulated = carry
        scores = jnp.einsum(
            "thl,kl->htk", query_latent, keys_latent, preferred_element_type=jnp.float32
        )
        scores = (
            scores
            + jnp.einsum(
                "thr,kr->htk", query_rotated, keys_rotated, preferred_element_type=jnp.float32
            )
        ) * score_scale
        allowed = key_valid[None, None, :] & (
            key_positions[None, None, :] <= positions[None, :, None]
        )
        scores = jnp.where(allowed, scores, -jnp.inf)
        new_highest = jnp.maximum(highest, jnp.max(scores, axis=2))
        fading = jnp.exp(highest - new_highest)
        soft_weights = jnp.exp(scores - new_highest[:, :, None])
        totals = totals * fading + jnp.sum(soft_weights, axis=2)
        accumulated = accumulated * fading[:, :, None] + jnp.einsum(
            "htk,kl->htl",
            soft_weights.astype(jnp.bfloat16),
            keys_latent,
            preferred_element_type=jnp.float32,
        )
        return (new_highest, totals, accumulated)

    pool_size = page_table.shape[1]
    pool_index = jnp.arange(pool_size, dtype=jnp.int32)
    inverse = jnp.sum(
        jnp.where(page_table[0][None, :] == pool_index[:, None], pool_index[None, :], 0), axis=1
    )
    starting = (
        jnp.full((H, row_count), floor_score, dtype=jnp.float32),
        jnp.zeros((H, row_count), dtype=jnp.float32),
        jnp.zeros((H, row_count, latent_width), dtype=jnp.float32),
    )
    piece_latent = lax.all_gather(latent, "tok", axis=0, tiled=True)
    piece_rotated = lax.all_gather(key_rotated, "tok", axis=0, tiled=True)
    key_count = piece_latent.shape[0]
    key_positions = length + jnp.arange(key_count, dtype=jnp.int32)
    key_valid = jnp.ones((key_count,), dtype=bool)
    carried = lax.cond(
        jnp.int32(0) < first_row + row_count,
        lambda current: attend(current, piece_latent, piece_rotated, key_positions, key_valid),
        lambda current: current,
        starting,
    )
    piece = lax.all_gather(latent_cache, "tok", axis=1, tiled=True)
    page_count = piece.shape[1]
    page_size = piece.shape[2]
    flat_pages = piece[0].reshape(page_count * page_size, entry_width)
    page_key_positions = (
        inverse[:, None] * page_size + jnp.arange(page_size, dtype=jnp.int32)[None, :]
    ).reshape(-1)
    page_key_valid = page_key_positions < length
    highest, totals, accumulated = lax.cond(
        jnp.any(page_key_valid),
        lambda current: attend(
            current,
            flat_pages[:, :latent_width],
            flat_pages[:, latent_width:],
            page_key_positions,
            page_key_valid,
        ),
        lambda current: current,
        carried,
    )
    mixed = (accumulated / totals[:, :, None]).astype(jnp.bfloat16)
    head_out = jnp.einsum(
        "htl,lhv->thv", mixed, weights[:, :, NOPE:], preferred_element_type=jnp.float32
    ).astype(jnp.bfloat16)
    attended = jnp.dot(
        head_out.reshape(row_count, H * VD), out_proj, preferred_element_type=jnp.float32
    )
    residual = hidden[0].astype(jnp.float32) + attended
    normed = rms_scale(residual, norm_gain).astype(jnp.bfloat16)
    top_count = routes.shape[2]
    capacity = CAP
    expert_count = EXPERTS
    flat_routes = routes[0].reshape(-1)
    onehot = (flat_routes[:, None] == jnp.arange(expert_count, dtype=jnp.int32)[None, :]).astype(
        jnp.int32
    )
    slot_index = jnp.sum((jnp.cumsum(onehot, axis=0) - 1) * onehot, axis=1)
    target = flat_routes * capacity + slot_index
    placing = (
        target[:, None] == jnp.arange(expert_count * capacity, dtype=jnp.int32)[None, :]
    ).astype(jnp.bfloat16)
    placing = jnp.sum(placing.reshape(row_count, top_count, expert_count * capacity), axis=1)
    outgoing = lax.dot_general(
        placing, normed, (((0,), (0,)), ((), ())), preferred_element_type=jnp.float32
    ).astype(jnp.bfloat16)
    slabs_here = expert_in.shape[0]
    req_count = lax.axis_size("req")
    tok_count = lax.axis_size("tok")
    device_count = req_count * tok_count
    outgoing = jnp.repeat(
        outgoing.reshape(expert_count, 1, capacity, model_width), 2, axis=1
    ).reshape(device_count, slabs_here, capacity, model_width)
    hidden_half = expert_out.shape[1]
    slab_rows = lax.all_to_all(outgoing, ("req", "tok"), split_axis=0, concat_axis=0, tiled=True)[
        :, 0
    ].reshape(-1, model_width)
    projected = jnp.dot(slab_rows, expert_in[0], preferred_element_type=jnp.float32)
    active = (jax.nn.silu(projected[:, :hidden_half]) * projected[:, hidden_half:]).astype(
        jnp.bfloat16
    )
    slab_result = jnp.dot(active, expert_out[0], preferred_element_type=jnp.float32).astype(
        jnp.bfloat16
    )
    results = [slab_result.reshape(device_count, -1, model_width)]
    returned = lax.all_to_all(
        jnp.stack(results, axis=1), ("req", "tok"), split_axis=0, concat_axis=0, tiled=True
    )
    returned = returned.reshape(expert_count, 2, capacity, model_width).astype(jnp.float32)
    combined = (returned[:, 0] + returned[:, 1]).reshape(expert_count * capacity, model_width)
    picked = jnp.take(combined, target, axis=0).reshape(row_count, top_count, model_width)
    gate_values = route_gates[0]
    routed = jnp.zeros_like(residual)
    for route_index in range(top_count):
        routed = routed + gate_values[:, route_index, None] * picked[:, route_index]
    layer_out = (residual + routed).astype(jnp.bfloat16)
    return (layer_out[None], jnp.concatenate([latent, key_rotated], axis=1)[None])


def solution(mesh):
    placed = (
        P("req", "tok", None),
        P("req", "tok", None),
        P("req", "tok", None),
        P("req", "tok", None, None),
        P("req", None),
        P("req"),
        P("req", "tok", None),
        P("req", "tok", None),
        P(),
        P(),
        P(),
        P(),
        P(("req", "tok"), None, None),
        P(("req", "tok"), None, None),
    )
    return jax.shard_map(
        local,
        mesh=mesh,
        in_specs=placed,
        out_specs=(P("req", "tok", None), P("req", "tok", None)),
        check_vma=False,
    )
```

profile of v0, /device:TPU:4, one launch (start us, length us, event | category | flops | bytes accessed | tf_op | source)
XLA Modules:
  0.0 506.4 jit_solution(15914417559145275520)
XLA Ops:
  7.2 1.1 bitcast_convert_fusion.1
  8.4 1.5 multiply_convert_fusion.2
  10.0 0.7 all-gather.5.cloned.1.call-update
  10.7 0.8 copy.106
  11.5 0.1 reshape_squeeze.14
  11.6 0.1 eq.59
  11.8 6.5 %copy.96 = bf16[512,4096]{0,1:T(8,128)(2,1)} copy(bf16[512,4096]{1,0:T(8,128)(2,1)} %param.26) | data formatting | bytes 8388608 | tf_op args[8]
  18.9 0.1 select_reduce_fusion
  19.1 0.7 compare_reduce_fusion
  20.3 2.3 copy.98
  22.6 0.7 fusion.60
  23.3 3.5 reduce-window.6
  26.7 0.3 slice_reduce_fusion
  27.0 0.1 fusion.59
  27.2 0.1 reduce_sum.73
  27.4 0.2 multiply_cosine_fusion
  27.6 26.3 %all_gather.10 = bf16[2048,64]{0,1:T(8,128)(2,1)S(1)} all-gather(bf16[128,64]{0,1:T(8,128)(2,1)S(1)} %pad_maximum_fusion.1), channel_id=1, replica_groups=mesh['req'=8,'tok'=16] {'tok'}, dimensions={0}, use_global_device_ids=true | all-gather | bytes 278528 | tf_op jit(solution)/shard_map/all_gather | solution.py:118
  53.9 1.0 slice_convert_fusion
  55.0 0.5 compare_and_fusion.1
  55.6 1.1 fusion.37
  56.7 3.8 convert_bitcast_fusion
  60.6 37.9 %conditional.2 = (f32[16,128]{1,0:T(8,128)}, f32[16,128]{1,0:T(8,128)S(1)}, f32[16,128,512]{2,1,0:T(8,128)}) conditional(s32[]{:T(128)} %convert_element_type.89, () %tuple.23, (s32[]{:T(128)}, s32[2048]{0:T(1024)S(1)}, s32[128]{0:T(128)S(1)}, bf16[2048,512]{0,1:T(8,128)(2,1)}, bf16[128,16,512]{0,2,1:T(8,128)(2,1)}, ...), branch_computations={%region_3.4_spmd, %region_4.7_spmd} | conditional | flops 9161680896 | bytes 103924272 | solution.py:122
  60.6 6.9 %fusion.5 = f32[2048,128,16]{1,0,2:T(8,128)S(1)} fusion(bf16[128,16,512]{0,2,1:T(8,128)(2,1)} %get-tuple-element.154, bf16[2048,512]{0,1:T(8,128)(2,1)} %get-tuple-element.153), kind=kOutput, calls=%fused_computation.7 | convolution fusion | flops 4294967296 | bytes 20971520 | tf_op jit(solution)/shard_map/cond/branch_1_fun/thl,kl->htk/dot_general | solution.py:82
  67.5 0.7 broadcast_add_fusion.1
  68.1 0.3 broadcast_compare_fusion
  68.5 7.6 %fusion.64 = (f32[16,128]{1,0:T(8,128)S(1)}, f32[16,128,2048]{1,2,0:T(8,128)}) fusion(f32[2048,128,16]{1,0,2:T(8,128)S(1)} %fusion.5, bf16[128,16,64]{0,2,1:T(8,128)(2,1)S(1)} %get-tuple-element.54, bf16[2048,64]{0,1:T(8,128)(2,1)S(1)} %get-tuple-element.53, pred[128,2048]{0,1:T(8,128)(4,1)S(1)} %broadcast_compare_fusion), kind=kOutput, calls=%fused_computation.127 | convolution fusion | flops 553646080 | bytes 34349056 | tf_op jit(solution)/shard_map/cond/branch_1_fun/thr,kr->htk/dot_general | solution.py:87
  76.1 0.6 exponential_multiply_fusion
  76.7 8.2 %fusion.1 = f32[16,128]{1,0:T(8,128)S(1)} fusion(f32[16,128,2048]{1,2,0:T(8,128)} %get-tuple-element.175, f32[16,128]{1,0:T(8,128)} %get-tuple-element.197), kind=kLoop, calls=%fused_computation.4 | loop fusion | flops 8386560 | bytes 16793600 | tf_op jit(solution)/shard_map/cond/branch_1_fun/reduce_sum | solution.py:98
  84.8 0.7 fusion.13
  85.6 12.9 %broadcast_add_fusion = f32[16,128,512]{2,1,0:T(8,128)} fusion(f32[16,128]{1,0:T(8,128)S(1)} %get-tuple-element.168, bf16[2048,512]{0,1:T(8,128)(2,1)S(1)} %copy-done.11, f32[16,128,2048]{1,2,0:T(8,128)} %get-tuple-element.175, f32[16,128]{1,0:T(8,128)} %get-tuple-element.197), kind=kOutput, calls=%fused_computation.10 | convolution fusion | flops 4304404480 | bytes 23085056 | tf_op jit(solution)/shard_map/cond/branch_1_fun/htk,kl->htl/dot_general | solution.py:99
  98.5 9.2 %all-gather.5.cloned.1.call-done = bf16[1,16,128,576]{2,3,0,1:T(8,128)(2,1)} async-done(((bf16[1,1,128,576]{2,3,0,1:T(8,128)(2,1)}), bf16[1,16,128,576]{2,3,0,1:T(8,128)(2,1)}) %all-gather.5.cloned.1.call-update) | async-done | bytes 2359312 | tf_op jit(solution)/shard_map/all_gather | solution.py:128
  107.8 45.9 %conditional.3 = ((f32[16,128]{1,0:T(8,128)S(1)}, f32[16,128,512]{2,1,0:T(8,128)})) conditional(s32[]{:T(128)} %convert_element_type.88, (f32[16,128]{1,0:T(8,128)S(1)}, f32[16,128,512]{2,1,0:T(8,128)}) %tuple.25, (s32[16,128]{1,0:T(8,128)S(1)}, s32[16,128]{1,0:T(8,128)S(1)}, s32[]{:T(128)}, s32[16,128]{1,0:T(8,128)S(1)}, s32[128]{0:T(128)S(1)}, ...), branch_computations={%region_7.8_spmd, %region_8.11_spmd} | conditional | flops 9162989568 | bytes 114176560 | solution.py:136
  107.8 4.6 copy.103
  112.4 6.8 %fusion.21 = f32[2048,128,16]{1,0,2:T(8,128)S(1)} fusion(bf16[128,16,512]{0,2,1:T(8,128)(2,1)} %get-tuple-element.163, bf16[2048,576]{1,0:T(8,128)(2,1)} %bitcast.177), kind=kOutput, calls=%fused_computation.25 | convolution fusion | flops 4294967296 | bytes 20971520 | tf_op jit(solution)/shard_map/cond/branch_1_fun/thl,kl->htk/dot_general | solution.py:82
  119.1 0.7 fusion.22
  119.8 1.5 compare_and_fusion
  121.3 8.7 %fusion.65 = (f32[16,128]{1,0:T(8,128)S(1)}, f32[16,128,2048]{1,2,0:T(8,128)}) fusion(f32[2048,128,16]{1,0,2:T(8,128)S(1)} %fusion.21, bf16[128,16,64]{0,2,1:T(8,128)(2,1)S(1)} %get-tuple-element.64, bf16[2048,576]{1,0:T(8,128)(2,1)} %bitcast.178, pred[128,2048]{0,1:T(8,128)(4,1)S(1)} %compare_and_fusion), kind=kOutput, calls=%fused_computation.128 | convolution fusion | flops 553646080 | bytes 34611200 | tf_op jit(solution)/shard_map/cond/branch_1_fun/thr,kr->htk/dot_general | solution.py:87
  130.0 0.7 max.2
  130.7 8.2 %fusion.15 = f32[16,128]{1,0:T(8,128)S(1)} fusion(f32[16,128,2048]{1,2,0:T(8,128)} %get-tuple-element.177, f32[16,128]{1,0:T(8,128)S(1)} %max.2), kind=kLoop, calls=%fused_computation.20 | loop fusion | flops 8386560 | bytes 16793600 | tf_op jit(solution)/shard_map/cond/branch_1_fun/reduce_sum | solution.py:98
  138.9 0.7 multiply_add_fusion.1
  139.6 13.6 %multiply_add_fusion = f32[16,128,512]{2,1,0:T(8,128)} fusion(f32[16,128,512]{2,1,0:T(8,128)} %get-tuple-element.65, f32[16,128]{1,0:T(8,128)S(1)} %get-tuple-element.171, f32[16,128,2048]{1,2,0:T(8,128)} %get-tuple-element.177, f32[16,128]{1,0:T(8,128)S(1)} %max.2, bf16[2048,576]{1,0:T(8,128)(2,1)S(1)} %bitcast.179), kind=kOutput, calls=%fused_computation.23 | convolution fusion | flops 4305453056 | bytes 27279360 | tf_op jit(solution)/shard_map/cond/branch_1_fun/htk,kl->htl/dot_general | solution.py:99
  153.6 3.7 fusion.38
  157.4 4.8 multiply_reduce_fusion
  162.2 1.1 copy-done.2
  163.3 3.0 convolution_convert_fusion.1
  166.3 5.9 %reshape.294 = bf16[64,14,2048]{2,1,0:T(8,128)(2,1)} reshape(bf16[896,2048]{1,0:T(8,128)(2,1)} %convolution_convert_fusion.1) | data formatting | bytes 7340032 | tf_op jit(solution)/shard_map/reshape | solution.py:178
  172.1 6.8 %broadcast_in_dim.93 = bf16[64,1,2,14,2048]{4,3,2,0,1:T(8,128)(2,1)} broadcast(bf16[64,14,2048]{2,1,0:T(8,128)(2,1)} %reshape.294), dimensions={0,3,4} | broadcast | bytes 11010048 | tf_op jit(solution)/shard_map/broadcast_in_dim | solution.py:177
  178.9 104.1 %all_to_all.10 = bf16[128,1,14,2048]{3,2,1,0:T(8,128)(2,1)} all-to-all(bf16[128,1,14,2048]{3,2,1,0:T(8,128)(2,1)} %bitcast.176), channel_id=1, replica_groups=mesh['req'=8,'tok'=16] {'req','tok'}, dimensions={0} | all-to-all | bytes 14680064 | tf_op jit(solution)/shard_map/all_to_all | solution.py:181
  282.9 10.9 %reshape_squeeze.15 = bf16[1792,2048]{1,0:T(8,128)(2,1)} reshape(bf16[128,1,14,2048]{3,2,1,0:T(8,128)(2,1)} %all_to_all.10) | data formatting | bytes 14680064 | tf_op jit(solution)/shard_map/reshape;squeeze | solution.py:183
  293.8 15.4 %fusion.24 = f32[1792,1408]{0,1:T(8,128)S(1)} fusion(bf16[1792,2048]{1,0:T(8,128)(2,1)} %reshape_squeeze.15, bf16[1,2048,1408]{2,1,0:T(8,128)(2,1)} %param.30), kind=kOutput, calls=%fused_computation.38 | convolution fusion | flops 10334765056 | bytes 23199744 | tf_op jit(solution)/shard_map/dot_general | solution.py:184
  309.2 8.2 %convolution_convert_fusion = bf16[1792,2048]{1,0:T(8,128)(2,1)} fusion(bf16[1,704,2048]{2,1,0:T(8,128)(2,1)S(1)} %copy-done, f32[1792,1408]{0,1:T(8,128)S(1)} %fusion.24), kind=kOutput, calls=%fused_computation.36 | convolution fusion | flops 5178621952 | bytes 20316160 | tf_op jit(solution)/shard_map/dot_general | solution.py:188
  317.4 11.1 %stack_reshape.3 = bf16[128,1,14,2048]{3,2,0,1:T(8,128)(2,1)} reshape(bf16[1792,2048]{1,0:T(8,128)(2,1)} %convolution_convert_fusion) | data formatting | bytes 14680064 | tf_op jit(solution)/shard_map/stack;reshape | solution.py:193
  328.6 7.7 %all-to-all-start.1 = ((bf16[128,1,14,2048]{3,2,1,0:T(8,128)(2,1)}), bf16[128,1,14,2048]{3,2,1,0:T(8,128)(2,1)}, u32[]{:S(2)}, u32[]{:S(2)}) async-start(bf16[128,1,14,2048]{3,2,1,0:T(8,128)(2,1)} %bitcast.175), calls=%async_computation.1 | async-start | bytes 16777216 | tf_op jit(solution)/shard_map/all_to_all | solution.py:192
  336.3 0.1 copy.113
  336.4 0.1 mul.268
  336.6 0.7 maximum_bitcast_fusion
  337.3 103.7 %all-to-all-done.1 = bf16[128,1,14,2048]{3,2,1,0:T(8,128)(2,1)} async-done(((bf16[128,1,14,2048]{3,2,1,0:T(8,128)(2,1)}), bf16[128,1,14,2048]{3,2,1,0:T(8,128)(2,1)}, u32[]{:S(2)}, u32[]{:S(2)}) %all-to-all-start.1) | async-done | bytes 7340064 | tf_op jit(solution)/shard_map/all_to_all | solution.py:192
  441.0 11.2 %bitcast_convert_fusion = f32[64,2,14,2048]{3,2,1,0:T(8,128)} fusion(bf16[64,2,14,2048]{3,2,1,0:T(8,128)(2,1)} %bitcast.171), kind=kLoop, calls=%fused_computation.35 | loop fusion | flops 3670016 | bytes 22020096 | tf_op jit(solution)/shard_map/convert_element_type | solution.py:195
  452.2 11.7 %fusion.23 = f32[64,1,14,2048]{3,2,0,1:T(8,128)} fusion(f32[64,2,14,2048]{3,2,1,0:T(8,128)} %bitcast_convert_fusion), kind=kLoop, calls=%fused_computation.33 | loop fusion | flops 1835008 | bytes 22020096 | tf_op jit(solution)/shard_map/add | solution.py:196
  463.9 8.2 %add.177 = f32[896,2048]{1,0:T(8,128)} reshape(f32[64,1,14,2048]{3,2,0,1:T(8,128)} %fusion.23) | data formatting | bytes 14680064 | tf_op jit(solution)/shard_map/add | solution.py:196
  472.1 10.3 %gather_fusion = f32[768,2048]{1,0:T(8,128)} fusion(f32[896,2048]{1,0:T(8,128)} %add.177, s32[1024]{0:T(1024)S(1)} %pad_clamp_fusion), kind=kCustom, calls=%fused_computation | custom fusion | bytes 12585984 | tf_op jit(solution)/shard_map/jit(_take)/gather | solution.py:197
  482.4 7.8 %gather.7 = f32[128,6,2048]{2,1,0:T(8,128)} reshape(f32[768,2048]{1,0:T(8,128)} %gather_fusion) | data formatting | bytes 12582912 | tf_op jit(solution)/shard_map/jit(_take)/gather | solution.py:197
  490.2 7.8 %copy_select_fusion = f32[128,6,2048]{2,0,1:T(8,128)S(1)} fusion(f32[128,6,2048]{2,1,0:T(8,128)} %gather.7, pred[128,6]{0,1:T(8,128)(4,1)S(1)} %copy-done.9), kind=kLoop, calls=%fused_computation.37 | loop fusion | flops 1572864 | bytes 12583680 | tf_op jit(solution)/shard_map/jit(_take)/select_n | solution.py:197
  498.0 1.3 fusion.57
  (50 shorter events, 0.7 us)
Async XLA Ops:
  7.2 302.1 %copy-start = (bf16[1,704,2048]{2,1,0:T(8,128)(2,1)S(1)}, bf16[1,704,2048]{2,1,0:T(8,128)(2,1)}, u32[]{:S(2)}) copy-start(bf16[1,704,2048]{2,1,0:T(8,128)(2,1)} %param.31) | copy-start | bytes 8650756
  7.2 11.8 %copy-start.12 = (s32[1,16]{1,0:T(1,128)S(1)}, s32[1,16]{1,0:T(1,128)}, u32[]{:S(2)}) copy-start(s32[1,16]{1,0:T(1,128)} %param.22) | copy-start | bytes 196
  7.2 53.4 %all-gather.3.cloned.1.call-start = ((), (), s32[]{:S(2)}) async-start(), calls=%async_computation.2 | async-start | bytes 2228224 | tf_op jit(solution)/shard_map/all_gather | solution.py:117
  9.9 97.8 %all-gather.5.cloned.1.call-start = ((), (), s32[]{:S(2)}) async-start(), calls=%async_computation.3 | async-start | bytes 2506752 | tf_op jit(solution)/shard_map/all_gather | solution.py:128
  11.7 43.3 %copy-start.7 = (s32[1,128,6]{1,0,2:T(1,128)S(1)}, s32[1,128,6]{1,0,2:T(1,128)}, u32[]{:S(2)}) copy-start(s32[1,128,6]{1,0,2:T(1,128)} %param.24) | copy-start | bytes 9220
  76.7 8.9 %copy-start.11 = (bf16[2048,512]{0,1:T(8,128)(2,1)S(1)}, bf16[2048,512]{0,1:T(8,128)(2,1)}, u32[]{:S(2)}) copy-start(bf16[2048,512]{0,1:T(8,128)(2,1)} %get-tuple-element.153) | copy-start | bytes 6291460 | tf_op jit(solution)/shard_map/cond
  130.7 8.9 %copy-start.1 = (bf16[1,16,128,576]{3,2,1,0:T(8,128)(2,1)S(1)}, bf16[1,16,128,576]{3,2,1,0:T(8,128)(2,1)}, u32[]{:S(2)}) copy-start(bf16[1,16,128,576]{3,2,1,0:T(8,128)(2,1)} %copy.103) | copy-start | bytes 7077892 | tf_op jit(solution)/shard_map/cond
  153.6 3.7 copy-start.6
  157.4 5.9 %copy-start.5 = (bf16[128,896]{1,0:T(8,128)(2,1)S(1)}, bf16[128,896]{1,0:T(8,128)(2,1)}, u32[]{:S(2)}) copy-start(bf16[128,896]{1,0:T(8,128)(2,1)} %fusion.37) | copy-start | bytes 688132
  157.4 5.9 %copy-start.8 = (f32[2048]{0:T(1024)S(1)}, f32[2048]{0:T(1024)}, u32[]{:S(2)}) copy-start(f32[2048]{0:T(1024)} %param.29) | copy-start | bytes 24580
  162.2 1.1 copy-start.2
  328.6 8.0 %copy-start.10 = (f32[1,128,6]{1,0,2:T(1,128)S(1)}, f32[1,128,6]{1,0,2:T(1,128)}, u32[]{:S(2)}) copy-start(f32[1,128,6]{1,0,2:T(1,128)} %param.25) | copy-start | bytes 9220
  328.6 8.0 %copy-start.4 = (bf16[128,512]{0,1:T(8,128)(2,1)S(1)}, bf16[128,512]{0,1:T(8,128)(2,1)}, u32[]{:S(2)}) copy-start(bf16[128,512]{0,1:T(8,128)(2,1)} %multiply_convert_fusion.2) | copy-start | bytes 393220
  328.6 112.4 %all-to-all-start.1 = ((bf16[128,1,14,2048]{3,2,1,0:T(8,128)(2,1)}), bf16[128,1,14,2048]{3,2,1,0:T(8,128)(2,1)}, u32[]{:S(2)}, u32[]{:S(2)}) async-start(bf16[128,1,14,2048]{3,2,1,0:T(8,128)(2,1)} %bitcast.175), calls=%async_computation.1 | async-start | bytes 16777216 | tf_op jit(solution)/shard_map/all_to_all | solution.py:192
  482.4 7.8 %copy-start.9 = (pred[128,6]{0,1:T(8,128)(4,1)S(1)}, pred[128,6]{0,1:T(8,128)(4,1)}, u32[]{:S(2)}) copy-start(pred[128,6]{0,1:T(8,128)(4,1)} %get-tuple-element.172) | copy-start | bytes 2308
  490.2 7.8 %copy-start.3 = (f32[128,2048]{1,0:T(8,128)S(1)}, f32[128,2048]{1,0:T(8,128)}, u32[]{:S(2)}) copy-start(f32[128,2048]{1,0:T(8,128)} %copy-done.2) | copy-start | bytes 3145732
Sparse Core Ops, SparseCore 0:
  10.7 49.8 all-gather.2
  62.7 44.9 all-gather.4
where the time goes:
time: 515 us; the launch traced here: 506 us
  blocking collectives  130 us (25%)
  waiting for transfers between devices  114 us (22%)
  matrix products  95.4 us (19%)
  local copies, waits for them, and re-layouts  77.3 us (15%)
  other arithmetic  65.7 us (13%)
  between operations  15.8 us (3%)
  starting transfers between devices  7.76 us (2%)
    all_to_all x1, blocking collectives, local(): lax.all_to_all(outgoing, ('req', 'tok'), split_axis=0, concat_axis=0, til...  104 us
    all_to_all x1, waiting for transfers between devices, local(): lax.all_to_all(jnp.stack(results, axis=1), ('req', 'tok'), split_axis=0,...  104 us
    dot_general x2, matrix products, attend(): jnp.einsum('htk,kl->htl', soft_weights.astype(jnp.bfloat16), keys_latent,...  26.5 us
    all_gather x1, blocking collectives, local(): piece_rotated = lax.all_gather(key_rotated, 'tok', axis=0, tiled=True)  26.3 us
    gather x2, local copies, waits for them, and re-layouts, local(): jnp.take(combined, target, axis=0)  18.2 us
    reduce_sum x2, other arithmetic, attend(): totals = totals * fading + jnp.sum(soft_weights, axis=2)  16.3 us
    dot_general x2, matrix products, attend(): jnp.einsum('thr,kr->htk', query_rotated, keys_rotated, preferred_element_...  16.3 us
    dot_general x1, matrix products, local(): jnp.dot(slab_rows, expert_in[0], preferred_element_type=jnp.float32)  15.4 us
  transfers between devices with their start and end apart: 3, of which 3 were waited for; matrix products, arithmetic and copies ran while one was open for 12% of the time, Pallas kernels for 0%

commit v1 on v0

v1 whole, which is shorter than its diff:
```python
import math

import jax
import jax.numpy as jnp
from jax import lax
from jax.experimental import pallas as pl
from jax.experimental.pallas import tpu as pltpu
from jax.sharding import PartitionSpec as P

H = 16
NOPE = 128
ROPE = 64
VD = 128
LAT = 512
EXPERTS = 64
SLOTS = 16
TOP = 6
BIG = 1 << 29

epsilon = 1e-06
theta_base = 10000.0
floor_score = -1e30
f32 = jnp.float32
bf16 = jnp.bfloat16


def rms_scale(values, gain):
    return values * lax.rsqrt(jnp.mean(values * values, axis=-1, keepdims=True) + epsilon) * gain


def turn(values, cosine, sine):
    half = values.shape[-1] // 2
    swapped = jnp.concatenate([values[:, half:], values[:, :half]], axis=-1)
    return values * cosine + swapped * sine


def dot(a, b):
    return jnp.dot(a, b, preferred_element_type=f32)


def dot_t(a, b):
    return lax.dot_general(a, b, (((1,), (1,)), ((), ())), preferred_element_type=f32)


def iota(shape, axis):
    return lax.broadcasted_iota(jnp.int32, shape, axis)


KB = 512
RB = 512


def attention_kernel(
    hidden, queries, cosine, sine, pages, fresh, krel, kv_up_hbm, out_proj_hbm, norm_gain, routes_t,
    residual_out, packed_out,
    kv_up, out_proj, ql, qr, acc, top, tot, heads, normed, packed, sems,
):
    rows = hidden.shape[0]
    first = lax.axis_index("tok") * rows
    load_up = pltpu.make_async_copy(kv_up_hbm, kv_up, sems.at[0])
    load_up.start()
    load_proj = pltpu.make_async_copy(out_proj_hbm, out_proj, sems.at[1])
    load_proj.start()
    width = NOPE + ROPE
    cos = cosine[...]
    sin = sine[...]
    for h in range(H):
        part = queries[:, h * width + NOPE : (h + 1) * width].astype(f32)
        qr[h * rows : (h + 1) * rows, :] = turn(part, cos, sin).astype(bf16)
    load_up.wait()
    for h in range(H):
        ql[h * rows : (h + 1) * rows, :] = dot_t(
            queries[:, h * width : h * width + NOPE], kv_up[:, h * 256 : h * 256 + NOPE]
        ).astype(bf16)
    top[...] = jnp.full_like(top, floor_score)
    tot[...] = jnp.zeros_like(tot)
    acc[...] = jnp.zeros_like(acc)
    scale = math.log2(math.e) / math.sqrt(width)
    qrel = first + lax.rem(iota((RB, KB), 0), rows)
    pages_per = KB // pages.shape[1]
    page_blocks = pages.shape[0] // pages_per

    def attend(keys_ref, block, rel_block):
        keys = keys_ref[pl.ds(block * pages_per, pages_per)].reshape(KB, LAT + ROPE)
        latent = keys[:, :LAT]
        rotated = keys[:, LAT:]
        allowed = krel[rel_block] <= qrel

        def scores(r):
            at = slice(r * RB, (r + 1) * RB)
            s = dot_t(ql[at, :], latent) + dot_t(qr[at, :], rotated)
            return jnp.where(allowed, s, floor_score)

        count = (H * rows) // RB
        current = scores(0)
        for r in range(count):
            following = scores(r + 1) if r + 1 < count else None
            at = slice(r * RB, (r + 1) * RB)
            before = top[at, :]
            now = jnp.maximum(before, jnp.max(current, axis=1, keepdims=True))
            fading = jnp.exp2((before - now) * scale)
            soft = jnp.exp2((current - jnp.tile(now, (1, KB // 128))) * scale)
            top[at, :] = now
            partial = soft[:, :128]
            for c in range(1, KB // 128):
                partial = partial + soft[:, c * 128 : (c + 1) * 128]
            tot[at, :] = tot[at, :] * fading + partial
            acc[at, :] = acc[at, :] * jnp.tile(fading, (1, LAT // 128)) + dot(soft.astype(bf16), latent)
            current = following

    def new_step(b, carry):
        attend(fresh, b, b)
        return carry

    def old_step(b, carry):
        attend(pages, b, b + page_blocks)
        return carry

    lax.fori_loop(0, page_blocks, new_step, 0)
    lax.fori_loop(0, page_blocks, old_step, 0)
    for h in range(H):
        at = slice(h * rows, (h + 1) * rows)
        total = jnp.sum(tot[at, :], axis=1, keepdims=True)
        mixed = (acc[at, :] / total).astype(bf16)
        heads[:, h * VD : (h + 1) * VD] = dot(
            mixed, kv_up[:, h * 256 + NOPE : (h + 1) * 256]
        ).astype(bf16)
    load_proj.wait()
    residual = hidden[...].astype(f32) + dot(heads[...], out_proj[...])
    residual_out[...] = residual
    normed[...] = rms_scale(residual, norm_gain[...]).astype(bf16)
    chosen = jnp.zeros((EXPERTS, rows), f32)
    for k in range(TOP):
        chosen = chosen + jnp.where(routes_t[k : k + 1, :] == iota((EXPERTS, rows), 0), 1.0, 0.0)
    earlier = jnp.where(iota((rows, rows), 0) < iota((rows, rows), 1), 1.0, 0.0).astype(bf16)
    rank = dot(chosen.astype(bf16), earlier)
    slot = jnp.where(chosen > 0.5, rank, -1.0)
    total_rows = EXPERTS * SLOTS
    spread = jnp.where(
        iota((total_rows, EXPERTS), 0) // SLOTS == iota((total_rows, EXPERTS), 1), 1.0, 0.0
    ).astype(bf16)
    slot_rows = dot(spread, slot.astype(bf16))
    wanted = lax.rem(iota((total_rows, rows), 0), SLOTS).astype(f32)
    placing = jnp.where(slot_rows == wanted, 1.0, 0.0).astype(bf16)
    packed[...] = dot(placing, normed[...]).astype(bf16).reshape(packed.shape)
    copies = [pltpu.make_async_copy(packed, packed_out.at[:, s], sems.at[s]) for s in range(2)]
    for copy in copies:
        copy.start()
    for copy in copies:
        copy.wait()


def expert_kernel(rows_ref, w_in, w_out, out_ref):
    half = w_out.shape[0]
    x = rows_ref[...].reshape(-1, rows_ref.shape[-1])
    g = dot(x, w_in[:, :half])
    u = dot(x, w_in[:, half:])
    active = (g / (1.0 + jnp.exp(-g)) * u).astype(bf16)
    out_ref[...] = dot(active, w_out[...]).astype(bf16).reshape(out_ref.shape)


def combine_kernel(returned, residual, routes, gates, out_ref, acc):
    step = pl.program_id(0)
    rows = residual.shape[0]
    group = returned.shape[0]
    width = group * SLOTS

    @pl.when(step == 0)
    def _():
        acc[...] = residual[...]

    expert = iota((rows, group), 1) + step * group
    chosen = jnp.zeros((rows, group), f32)
    gate = jnp.zeros((rows, group), f32)
    for k in range(TOP):
        hit = routes[:, k : k + 1] == expert
        chosen = chosen + jnp.where(hit, 1.0, 0.0)
        gate = gate + jnp.where(hit, gates[:, k : k + 1], 0.0)
    earlier = jnp.where(iota((rows, rows), 1) < iota((rows, rows), 0), 1.0, 0.0).astype(bf16)
    slot = jnp.where(chosen > 0.5, dot(earlier, chosen.astype(bf16)), -1.0)
    spread = jnp.where(
        iota((group, width), 1) // SLOTS == iota((group, width), 0), 1.0, 0.0
    ).astype(bf16)
    slot_cols = dot(slot.astype(bf16), spread)
    match = slot_cols == lax.rem(iota((rows, width), 1), SLOTS).astype(f32)
    high = gate.astype(bf16)
    low = (gate - high.astype(f32)).astype(bf16)
    weight_high = jnp.where(match, dot(high, spread), 0.0).astype(bf16)
    weight_low = jnp.where(match, dot(low, spread), 0.0).astype(bf16)
    total = acc[...]
    for s in range(2):
        block = returned[:, s].reshape(width, -1)
        total = total + dot(weight_high, block) + dot(weight_low, block)
    acc[...] = total

    @pl.when(step == pl.num_programs(0) - 1)
    def _():
        out_ref[...] = total.astype(bf16)


def local(
    hidden,
    queries,
    fresh_latent,
    latent_cache,
    page_table,
    cache_lengths,
    routes,
    route_gates,
    kv_up,
    out_proj,
    latent_gain,
    norm_gain,
    expert_in,
    expert_out,
):
    rows, width = hidden.shape[1:]
    pool = page_table.shape[1]
    page = latent_cache.shape[2]
    entry = latent_cache.shape[3]
    devices = lax.axis_size("req") * lax.axis_size("tok")
    length = cache_lengths[0]
    positions = length + lax.axis_index("tok") * rows + jnp.arange(rows, dtype=jnp.int32)
    frequency = theta_base ** (-jnp.arange(ROPE // 2, dtype=f32) * 2.0 / ROPE)
    angles = positions.astype(f32)[:, None] * frequency[None, :]
    cos = jnp.cos(angles)
    sin = jnp.sin(angles)
    cosine = jnp.concatenate([cos, cos], axis=1)
    sine = jnp.concatenate([-sin, sin], axis=1)
    raw = fresh_latent[0].astype(f32)
    latent = rms_scale(raw[:, :LAT], latent_gain).astype(bf16)
    key_rotated = turn(raw[:, LAT:], cosine, sine).astype(bf16)
    new_latent = jnp.concatenate([latent, key_rotated], axis=1)
    pages = lax.all_gather(latent_cache[0], "tok", axis=0, tiled=True)
    fresh = lax.all_gather(new_latent[None], "tok", axis=0, tiled=True)
    pool_index = jnp.arange(pool, dtype=jnp.int32)
    inverse = jnp.sum(
        jnp.where(page_table[0][None, :] == pool_index[:, None], pool_index[None, :], 0), axis=1
    )
    old_positions = (inverse[:, None] * page + jnp.arange(page, dtype=jnp.int32)[None, :]).reshape(-1)
    old_rel = jnp.where(old_positions < length, -1, BIG)
    krel = jnp.concatenate([jnp.arange(pool * rows, dtype=jnp.int32), old_rel]).reshape(-1, 1, KB)

    vmem = pl.BlockSpec(memory_space=pltpu.VMEM)
    anywhere = pl.BlockSpec(memory_space=pl.ANY)
    residual, packed = pl.pallas_call(
        attention_kernel,
        out_shape=(
            jax.ShapeDtypeStruct((rows, width), f32),
            jax.ShapeDtypeStruct((EXPERTS, 2, SLOTS, width), bf16),
        ),
        in_specs=[vmem] * 7 + [anywhere, anywhere, vmem, vmem],
        out_specs=(vmem, anywhere),
        scratch_shapes=[
            pltpu.VMEM(kv_up.shape, bf16),
            pltpu.VMEM(out_proj.shape, bf16),
            pltpu.VMEM((H * rows, LAT), bf16),
            pltpu.VMEM((H * rows, ROPE), bf16),
            pltpu.VMEM((H * rows, LAT), f32),
            pltpu.VMEM((H * rows, 128), f32),
            pltpu.VMEM((H * rows, 128), f32),
            pltpu.VMEM((rows, H * VD), bf16),
            pltpu.VMEM((rows, width), bf16),
            pltpu.VMEM((EXPERTS, SLOTS, width), bf16),
            pltpu.SemaphoreType.DMA((2,)),
        ],
        compiler_params=pltpu.CompilerParams(vmem_limit_bytes=60 << 20),
        name="attention",
    )(
        hidden[0], queries[0], cosine, sine, pages, fresh, krel, kv_up, out_proj,
        norm_gain[None], routes[0].T,
    )
    sent = packed.reshape(devices, SLOTS, width)
    arrived = lax.all_to_all(sent, ("req", "tok"), split_axis=0, concat_axis=0, tiled=True)
    steps = 8
    block = pl.BlockSpec((devices // steps, SLOTS, width), lambda i: (i, 0, 0))
    results = pl.pallas_call(
        expert_kernel,
        out_shape=jax.ShapeDtypeStruct((devices, SLOTS, width), bf16),
        grid=(steps,),
        in_specs=[
            block,
            pl.BlockSpec(expert_in.shape[1:], lambda i: (0, 0), pipeline_mode=pl.Buffered(1)),
            pl.BlockSpec(expert_out.shape[1:], lambda i: (0, 0), pipeline_mode=pl.Buffered(1)),
        ],
        out_specs=block,
        compiler_params=pltpu.CompilerParams(vmem_limit_bytes=60 << 20),
        name="experts",
    )(arrived, expert_in[0], expert_out[0])
    returned = lax.all_to_all(results, ("req", "tok"), split_axis=0, concat_axis=0, tiled=True)
    groups = 4
    layer_out = pl.pallas_call(
        combine_kernel,
        out_shape=jax.ShapeDtypeStruct((rows, width), bf16),
        grid=(groups,),
        in_specs=[
            pl.BlockSpec((EXPERTS // groups, 2, SLOTS, width), lambda i: (i, 0, 0, 0)),
            pl.BlockSpec((rows, width), lambda i: (0, 0)),
            pl.BlockSpec((rows, TOP), lambda i: (0, 0)),
            pl.BlockSpec((rows, TOP), lambda i: (0, 0)),
        ],
        out_specs=pl.BlockSpec((rows, width), lambda i: (0, 0)),
        scratch_shapes=[pltpu.VMEM((rows, width), f32)],
        compiler_params=pltpu.CompilerParams(vmem_limit_bytes=60 << 20),
        name="combine",
    )(returned.reshape(EXPERTS, 2, SLOTS, width), residual, routes[0], route_gates[0])
    return (layer_out[None], new_latent[None])


def solution(mesh):
    placed = (
        P("req", "tok", None),
        P("req", "tok", None),
        P("req", "tok", None),
        P("req", "tok", None, None),
        P("req", None),
        P("req"),
        P("req", "tok", None),
        P("req", "tok", None),
        P(),
        P(),
        P(),
        P(),
        P(("req", "tok"), None, None),
        P(("req", "tok"), None, None),
    )
    return jax.shard_map(
        local,
        mesh=mesh,
        in_specs=placed,
        out_specs=(P("req", "tok", None), P("req", "tok", None)),
        check_vma=False,
    )
```

time: 515 us -> 405 us (0.79)
  the two profiles are of different devices: /device:TPU:4 before, /device:TPU:31 now
where the time goes in v1:
time: 405 us; the launch traced here: 400 us
  waiting for transfers between devices  184 us (45%)
  blocking collectives  105 us (26%)
  Pallas kernels  74.8 us (18%)
  between operations  14.8 us (4%)
  local copies, waits for them, and re-layouts  9.14 us (2%)
  starting transfers between devices  7.73 us (2%)
  other arithmetic  4.1 us (1%)
    all_to_all x1, blocking collectives, local(): lax.all_to_all(sent, ('req', 'tok'), split_axis=0, concat_axis=0, tiled=T...  105 us
    all_to_all x1, waiting for transfers between devices, local(): lax.all_to_all(results, ('req', 'tok'), split_axis=0, concat_axis=0, tile...  98.4 us
    all_gather x1, waiting for transfers between devices, local(): fresh = lax.all_gather(new_latent[None], 'tok', axis=0, tiled=True)  44.5 us
    pallas_call x1, Pallas kernels, local(): pl.pallas_call(attention_kernel, out_shape=(jax.ShapeDtypeStruct((rows, w...  40.9 us
    all_gather x1, waiting for transfers between devices, local(): pages = lax.all_gather(latent_cache[0], 'tok', axis=0, tiled=True)  40.1 us
    pallas_call x1, Pallas kernels, local(): pl.pallas_call(expert_kernel, out_shape=jax.ShapeDtypeStruct((devices, SL...  25.9 us
  transfers between devices with their start and end apart: 3, of which 3 were waited for; matrix products, arithmetic and copies ran while one was open for 3% of the time, Pallas kernels for 0%

profile of v1, /device:TPU:31, one launch (start us, length us, event | category | flops | bytes accessed | tf_op | source)
XLA Modules:
  0.0 399.7 jit_solution(5150786677526826258)
XLA Ops:
  7.2 0.0 all-gather.5.cloned.1.call-start
  7.2 0.7 all-gather.5.cloned.1.call-update
  7.9 0.0 all-gather.7.cloned.1.call-start
  7.9 1.1 copy.36
  9.7 0.1 multiply_reduce_fusion
  9.9 0.3 fusion.2
  10.2 0.8 fusion.1
  11.0 0.8 multiply_convert_fusion
  11.7 0.7 fusion.3
  12.4 0.0 all-gather.7.cloned.1.call-update
  12.4 0.8 select_reduce_fusion
  13.2 0.1 mul.67
  13.3 1.3 copy.43
  14.6 0.1 add.68
  14.7 0.6 pad_add_fusion.krel
  15.3 40.1 %all-gather.5.cloned.1.call-done = bf16[16,1,128,576]{2,3,1,0:T(8,128)(2,1)} async-done(((bf16[1,1,128,576]{2,3,1,0:T(8,128)(2,1)}), bf16[16,1,128,576]{2,3,1,0:T(8,128)(2,1)}) %all-gather.5.cloned.1.call-update) | async-done | bytes 2359312 | tf_op jit(solution)/shard_map/all_gather | solution.py:234
  55.3 4.4 %copy.35 = bf16[16,1,128,576]{3,2,0,1:T(8,128)(2,1)} copy(bf16[16,1,128,576]{2,3,1,0:T(8,128)(2,1)} %all-gather.5.cloned.1.call-done) | data formatting | bytes 4718592 | tf_op jit(solution)/shard_map/all_gather | solution.py:234
  59.7 44.5 %all-gather.7.cloned.1.call-done = bf16[2048,576]{1,0:T(8,128)(2,1)} async-done(((bf16[128,576]{1,0:T(8,128)(2,1)}), bf16[2048,576]{1,0:T(8,128)(2,1)}) %all-gather.7.cloned.1.call-update) | async-done | bytes 2359312 | tf_op jit(solution)/shard_map/all_gather | solution.py:235
  104.2 40.9 %attention.1 = (f32[128,2048]{1,0:T(8,128)}, bf16[64,2,16,2048]{3,2,1,0:T(8,128)(2,1)}) custom-call(bf16[128,2048]{1,0:T(8,128)(2,1)} %bitcast.34, bf16[128,3072]{1,0:T(8,128)(2,1)} %bitcast.33, f32[128,64]{1,0:T(8,128)} %get-tuple-element.20.cosine, f32[128,64]{1,0:T(8,128)} %get-tuple-element.15.sine, bf16[16,128,576]{2,1,0:T(8,128)(2,1)} %bitcast.28, ...), custom_call_target="tpu_custom_call" | custom-call | tf_op jit(solution)/shard_map/attention/pallas_call | solution.py:246
  145.2 105.5 %all_to_all.10.rows_ref = bf16[128,16,2048]{2,1,0:T(8,128)(2,1)} all-to-all(bf16[128,16,2048]{2,1,0:T(8,128)(2,1)} %bitcast.29), channel_id=1, replica_groups=mesh['req'=8,'tok'=16] {'req','tok'}, dimensions={0} | all-to-all | bytes 16777216 | tf_op jit(solution)/shard_map/all_to_all | solution.py:274
  250.6 25.9 %experts.1 = bf16[128,16,2048]{2,1,0:T(8,128)(2,1)} custom-call(bf16[128,16,2048]{2,1,0:T(8,128)(2,1)} %all_to_all.10.rows_ref, bf16[2048,1408]{1,0:T(8,128)(2,1)} %bitcast.30, bf16[704,2048]{1,0:T(8,128)(2,1)} %bitcast.31), custom_call_target="tpu_custom_call" | custom-call | tf_op jit(solution)/shard_map/experts/pallas_call | solution.py:277
  276.5 0.0 copy-start
  276.5 0.0 copy-start.1
  276.5 7.7 %all-to-all-start.1 = ((bf16[128,16,2048]{2,1,0:T(8,128)(2,1)}), bf16[128,16,2048]{2,1,0:T(8,128)(2,1)}, u32[]{:S(2)}, u32[]{:S(2)}) async-start(bf16[128,16,2048]{2,1,0:T(8,128)(2,1)} %experts.1), calls=%async_computation.1 | async-start | bytes 16777216 | tf_op jit(solution)/shard_map/all_to_all | solution.py:290
  284.2 0.0 copy-done
  284.2 0.7 copy.37
  284.9 0.0 copy-done.1
  284.9 0.7 copy.39
  285.7 0.8 copy.40
  286.4 98.4 %all-to-all-done.1 = bf16[128,16,2048]{2,1,0:T(8,128)(2,1)} async-done(((bf16[128,16,2048]{2,1,0:T(8,128)(2,1)}), bf16[128,16,2048]{2,1,0:T(8,128)(2,1)}, u32[]{:S(2)}, u32[]{:S(2)}) %all-to-all-start.1) | async-done | bytes 8388640 | tf_op jit(solution)/shard_map/all_to_all | solution.py:290
  384.8 8.0 %combine.1 = bf16[128,2048]{1,0:T(8,128)(2,1)} custom-call(bf16[64,2,16,2048]{3,2,1,0:T(8,128)(2,1)} %bitcast.17.returned, f32[128,2048]{1,0:T(8,128)} %get-tuple-element.5.residual, s32[128,6]{1,0:T(8,128)} %bitcast.36, f32[128,6]{1,0:T(8,128)} %bitcast.37), custom_call_target="tpu_custom_call" | custom-call | tf_op jit(solution)/shard_map/combine/pallas_call | solution.py:292
  (7 shorter events, 0.1 us)
Async XLA Ops:
  7.2 48.2 %all-gather.5.cloned.1.call-start = ((), (), s32[]{:S(2)}) async-start(), calls=%async_computation.2 | async-start | bytes 2506752 | tf_op jit(solution)/shard_map/all_gather | solution.py:234
  7.9 96.3 %all-gather.7.cloned.1.call-start = ((), (), s32[]{:S(2)}) async-start(), calls=%async_computation.3 | async-start | bytes 2785280 | tf_op jit(solution)/shard_map/all_gather | solution.py:235
  276.5 7.7 %copy-start = (s32[1,128,6]{1,0,2:T(1,128)S(1)}, s32[1,128,6]{1,0,2:T(1,128)}, u32[]{:S(2)}) copy-start(s32[1,128,6]{1,0,2:T(1,128)} %param.20) | copy-start | bytes 9220
  276.5 8.4 %copy-start.1 = (f32[1,128,6]{1,0,2:T(1,128)S(1)}, f32[1,128,6]{1,0,2:T(1,128)}, u32[]{:S(2)}) copy-start(f32[1,128,6]{1,0,2:T(1,128)} %param.21) | copy-start | bytes 9220
  276.5 108.3 %all-to-all-start.1 = ((bf16[128,16,2048]{2,1,0:T(8,128)(2,1)}), bf16[128,16,2048]{2,1,0:T(8,128)(2,1)}, u32[]{:S(2)}, u32[]{:S(2)}) async-start(bf16[128,16,2048]{2,1,0:T(8,128)(2,1)} %experts.1), calls=%async_computation.1 | async-start | bytes 16777216 | tf_op jit(solution)/shard_map/all_to_all | solution.py:290
Sparse Core Ops, SparseCore 0:
  10.1 45.1 all-gather.4
  58.1 46.1 all-gather.6

commit v2 on v1

--- a/solution.py
+++ b/solution.py
@@ -46,27 +46,124 @@
     return lax.broadcasted_iota(jnp.int32, shape, axis)
 
 
-KB = 512
+KB = 256
 RB = 512
+SIDE = 4
+MOVES = 36
+ENTRY = 2 * (LAT + ROPE)
+
+
+def pick(step, values):
+    chosen = values[0]
+    for n in range(1, len(values)):
+        chosen = jnp.where(step == n, values[n], chosen)
+    return chosen
 
 
 def attention_kernel(
-    hidden, queries, cosine, sine, pages, fresh, krel, kv_up_hbm, out_proj_hbm, norm_gain, routes_t,
+    hidden, queries, cosine, sine, own, old_rel, kv_up_hbm, out_proj_hbm, norm_gain, routes_t,
     residual_out, packed_out,
-    kv_up, out_proj, ql, qr, acc, top, tot, heads, normed, packed, sems,
+    kv, kv_up, out_proj, ql, qr_old, qr_new, acc, top, tot, heads, normed, packed,
+    sems, send_sems, recv_sems,
 ):
     rows = hidden.shape[0]
-    first = lax.axis_index("tok") * rows
+    me = lax.axis_index("tok")
+    my_z = me // SIDE
+    my_y = lax.rem(me, SIDE)
+    first = me * rows
+
+    def at_offset(dy, dz):
+        return lax.rem(my_z + dz + SIDE, SIDE) * SIDE + lax.rem(my_y + dy + SIDE, SIDE)
+
+    def offset(axis, sign):
+        return (sign, 0) if axis == "y" else (0, sign)
+
+    directions = [("y", 1), ("y", -1), ("z", 1), ("z", -1)]
     load_up = pltpu.make_async_copy(kv_up_hbm, kv_up, sems.at[0])
     load_up.start()
     load_proj = pltpu.make_async_copy(out_proj_hbm, out_proj, sems.at[1])
     load_proj.start()
+    keep = pltpu.make_async_copy(own, kv.at[me], sems.at[2])
+    keep.start()
+
+    barrier = pltpu.get_barrier_semaphore()
+    for axis, sign in directions:
+        pl.semaphore_signal(
+            barrier,
+            inc=1,
+            device_id={"tok": at_offset(*offset(axis, sign))},
+            device_id_type=pl.DeviceIdType.MESH,
+        )
+    pl.semaphore_wait(barrier, len(directions))
+
+    def move(number, source, block, row, count, axis, sign):
+        target = at_offset(*offset(axis, sign))
+        return pltpu.make_async_remote_copy(
+            src_ref=source.at[pl.ds(row, count)],
+            dst_ref=kv.at[block, pl.ds(row, count)],
+            send_sem=send_sems.at[number],
+            recv_sem=recv_sems.at[number],
+            device_id={"tok": target},
+            device_id_type=pl.DeviceIdType.MESH,
+        )
+
+    quarter = rows // 4
+    plans = [[], [], [], []]
+    for axis, sign in directions:
+        plans[0].append((None, 0, rows, axis, sign))
+    for axis, sign in directions:
+        back = offset(axis, -sign)
+        start = 0 if sign > 0 else quarter
+        plans[1].append((back, start, quarter, axis, sign))
+        plans[1].append((back, start + 2 * quarter, quarter, axis, sign))
+        for other in (1, -1):
+            side = (other, 0) if axis == "z" else (0, other)
+            plans[1].append((side, 0 if axis == "z" else 2 * quarter, 2 * quarter, axis, sign))
+    for axis, sign in directions:
+        far = (2, 0) if axis == "z" else (0, 2)
+        half = 0 if axis == "z" else 2 * quarter
+        start = half + (0 if sign > 0 else quarter)
+        plans[2].append((far, half, 2 * quarter, axis, sign))
+        for other in (1, -1):
+            corner = (other, -sign) if axis == "z" else (-sign, other)
+            plans[2].append((corner, start, quarter, axis, sign))
+        corner = (2, -sign) if axis == "z" else (-sign, 2)
+        plans[3].append((corner, start, quarter, axis, sign))
+
+    first_number = [0]
+    for plan in plans:
+        first_number.append(first_number[-1] + len(plan))
+
+    def copies(level):
+        made = []
+        for n, (source, row, count, axis, sign) in enumerate(plans[level]):
+            if source is None:
+                block, ref = me, own
+            else:
+                block = at_offset(*source)
+                ref = kv.at[block]
+            made.append(move(first_number[level] + n, ref, block, row, count, axis, sign))
+        return made
+
+    def start_level(level):
+        for copy in copies(level):
+            copy.start()
+
+    def finish_level(level):
+        for copy in copies(level):
+            copy.wait()
+
+    start_level(0)
     width = NOPE + ROPE
     cos = cosine[...]
     sin = sine[...]
+    blank = jnp.zeros((rows, ROPE), bf16)
     for h in range(H):
+        at = slice(h * rows, (h + 1) * rows)
         part = queries[:, h * width + NOPE : (h + 1) * width].astype(f32)
-        qr[h * rows : (h + 1) * rows, :] = turn(part, cos, sin).astype(bf16)
+        turned = turn(part, cos, sin).astype(bf16)
+        qr_old[at, :] = jnp.concatenate([turned, blank], axis=1)
+        qr_new[at, :] = jnp.concatenate([blank, turned], axis=1)
     load_up.wait()
     for h in range(H):
         ql[h * rows : (h + 1) * rows, :] = dot_t(
@@ -77,19 +174,46 @@
     acc[...] = jnp.zeros_like(acc)
     scale = math.log2(math.e) / math.sqrt(width)
     qrel = first + lax.rem(iota((RB, KB), 0), rows)
-    pages_per = KB // pages.shape[1]
-    page_blocks = pages.shape[0] // pages_per
-
-    def attend(keys_ref, block, rel_block):
-        keys = keys_ref[pl.ds(block * pages_per, pages_per)].reshape(KB, LAT + ROPE)
-        latent = keys[:, :LAT]
-        rotated = keys[:, LAT:]
-        allowed = krel[rel_block] <= qrel
+    keep.wait()
+
+    order = [
+        (0, 0),
+        (1, 0), (-1, 0), (0, 1), (0, -1),
+        (2, 0), (0, 2), (1, 1), (1, -1), (-1, 1), (-1, -1),
+        (2, 1), (2, -1), (1, 2), (-1, 2),
+        (2, 2),
+    ]
+    pairs = len(order) // 2
+    level_at = {0: 0, 2: 1, 5: 2, 7: 3}
+
+    def attend(step, carry):
+        for when, level in level_at.items():
+
+            @pl.when(step == when)
+            def _():
+                finish_level(level)
+                if level + 1 < len(plans):
+                    start_level(level + 1)
+
+        one = pick(step, [at_offset(*order[2 * n]) for n in range(pairs)])
+        two = pick(step, [at_offset(*order[2 * n + 1]) for n in range(pairs)])
+        old = jnp.concatenate([kv[one, :, :LAT], kv[two, :, :LAT]], axis=0)
+        new = jnp.concatenate([kv[one, :, LAT : 2 * LAT], kv[two, :, LAT : 2 * LAT]], axis=0)
+        rotated = jnp.concatenate([kv[one, :, 2 * LAT :], kv[two, :, 2 * LAT :]], axis=0)
+        old_at = jnp.concatenate([old_rel[one], old_rel[two]], axis=1)
+        lane = iota((1, rows), 1)
+        new_at = jnp.concatenate([one * rows + lane, two * rows + lane], axis=1)
+        old_allowed = old_at <= qrel
+        new_allowed = new_at <= qrel
 
         def scores(r):
             at = slice(r * RB, (r + 1) * RB)
-            s = dot_t(ql[at, :], latent) + dot_t(qr[at, :], rotated)
-            return jnp.where(allowed, s, floor_score)
+            s_old = dot_t(ql[at, :], old) + dot_t(qr_old[at, :], rotated)
+            s_new = dot_t(ql[at, :], new) + dot_t(qr_new[at, :], rotated)
+            return (
+                jnp.where(old_allowed, s_old, floor_score),
+                jnp.where(new_allowed, s_new, floor_score),
+            )
 
         count = (H * rows) // RB
         current = scores(0)
@@ -97,27 +221,24 @@
             following = scores(r + 1) if r + 1 < count else None
             at = slice(r * RB, (r + 1) * RB)
             before = top[at, :]
-            now = jnp.maximum(before, jnp.max(current, axis=1, keepdims=True))
+            s_old, s_new = current
+            now = jnp.maximum(before, jnp.max(jnp.maximum(s_old, s_new), axis=1, keepdims=True))
             fading = jnp.exp2((before - now) * scale)
-            soft = jnp.exp2((current - jnp.tile(now, (1, KB // 128))) * scale)
+            wide = jnp.tile(now, (1, KB // 128))
+            soft_old = jnp.exp2((s_old - wide) * scale)
+            soft_new = jnp.exp2((s_new - wide) * scale)
             top[at, :] = now
-            partial = soft[:, :128]
-            for c in range(1, KB // 128):
-                partial = partial + soft[:, c * 128 : (c + 1) * 128]
-            tot[at, :] = tot[at, :] * fading + partial
-            acc[at, :] = acc[at, :] * jnp.tile(fading, (1, LAT // 128)) + dot(soft.astype(bf16), latent)
+            both = soft_old + soft_new
+            tot[at, :] = tot[at, :] * fading + both[:, :128] + both[:, 128:]
+            acc[at, :] = (
+                acc[at, :] * jnp.tile(fading, (1, LAT // 128))
+                + dot(soft_old.astype(bf16), old)
+                + dot(soft_new.astype(bf16), new)
+            )
             current = following
-
-    def new_step(b, carry):
-        attend(fresh, b, b)
         return carry
 
-    def old_step(b, carry):
-        attend(pages, b, b + page_blocks)
-        return carry
-
-    lax.fori_loop(0, page_blocks, new_step, 0)
-    lax.fori_loop(0, page_blocks, old_step, 0)
+    lax.fori_loop(0, pairs, attend, 0)
     for h in range(H):
         at = slice(h * rows, (h + 1) * rows)
         total = jnp.sum(tot[at, :], axis=1, keepdims=True)
@@ -143,10 +264,10 @@
     wanted = lax.rem(iota((total_rows, rows), 0), SLOTS).astype(f32)
     placing = jnp.where(slot_rows == wanted, 1.0, 0.0).astype(bf16)
     packed[...] = dot(placing, normed[...]).astype(bf16).reshape(packed.shape)
-    copies = [pltpu.make_async_copy(packed, packed_out.at[:, s], sems.at[s]) for s in range(2)]
-    for copy in copies:
+    outgoing = [pltpu.make_async_copy(packed, packed_out.at[:, s], sems.at[s]) for s in range(2)]
+    for copy in outgoing:
         copy.start()
-    for copy in copies:
+    for copy in outgoing:
         copy.wait()
 
 
@@ -217,7 +338,6 @@
     rows, width = hidden.shape[1:]
     pool = page_table.shape[1]
     page = latent_cache.shape[2]
-    entry = latent_cache.shape[3]
     devices = lax.axis_size("req") * lax.axis_size("tok")
     length = cache_lengths[0]
     positions = length + lax.axis_index("tok") * rows + jnp.arange(rows, dtype=jnp.int32)
@@ -231,15 +351,14 @@
     latent = rms_scale(raw[:, :LAT], latent_gain).astype(bf16)
     key_rotated = turn(raw[:, LAT:], cosine, sine).astype(bf16)
     new_latent = jnp.concatenate([latent, key_rotated], axis=1)
-    pages = lax.all_gather(latent_cache[0], "tok", axis=0, tiled=True)
-    fresh = lax.all_gather(new_latent[None], "tok", axis=0, tiled=True)
+    cached = latent_cache[0, 0]
+    own = jnp.concatenate([cached[:, :LAT], latent, cached[:, LAT:], key_rotated], axis=1)
     pool_index = jnp.arange(pool, dtype=jnp.int32)
     inverse = jnp.sum(
         jnp.where(page_table[0][None, :] == pool_index[:, None], pool_index[None, :], 0), axis=1
     )
-    old_positions = (inverse[:, None] * page + jnp.arange(page, dtype=jnp.int32)[None, :]).reshape(-1)
-    old_rel = jnp.where(old_positions < length, -1, BIG)
-    krel = jnp.concatenate([jnp.arange(pool * rows, dtype=jnp.int32), old_rel]).reshape(-1, 1, KB)
+    old_positions = inverse[:, None] * page + jnp.arange(page, dtype=jnp.int32)[None, :]
+    old_rel = jnp.where(old_positions < length, -1, BIG)[:, None, :]
 
     vmem = pl.BlockSpec(memory_space=pltpu.VMEM)
     anywhere = pl.BlockSpec(memory_space=pl.ANY)
@@ -249,25 +368,31 @@
             jax.ShapeDtypeStruct((rows, width), f32),
             jax.ShapeDtypeStruct((EXPERTS, 2, SLOTS, width), bf16),
         ),
-        in_specs=[vmem] * 7 + [anywhere, anywhere, vmem, vmem],
+        in_specs=[vmem] * 6 + [anywhere, anywhere, vmem, vmem],
         out_specs=(vmem, anywhere),
         scratch_shapes=[
+            pltpu.VMEM((pool, rows, ENTRY), bf16),
             pltpu.VMEM(kv_up.shape, bf16),
             pltpu.VMEM(out_proj.shape, bf16),
             pltpu.VMEM((H * rows, LAT), bf16),
-            pltpu.VMEM((H * rows, ROPE), bf16),
+            pltpu.VMEM((H * rows, 2 * ROPE), bf16),
+            pltpu.VMEM((H * rows, 2 * ROPE), bf16),
             pltpu.VMEM((H * rows, LAT), f32),
             pltpu.VMEM((H * rows, 128), f32),
             pltpu.VMEM((H * rows, 128), f32),
             pltpu.VMEM((rows, H * VD), bf16),
             pltpu.VMEM((rows, width), bf16),
             pltpu.VMEM((EXPERTS, SLOTS, width), bf16),
-            pltpu.SemaphoreType.DMA((2,)),
+            pltpu.SemaphoreType.DMA((3,)),
+            pltpu.SemaphoreType.DMA((MOVES,)),
+            pltpu.SemaphoreType.DMA((MOVES,)),
         ],
-        compiler_params=pltpu.CompilerParams(vmem_limit_bytes=60 << 20),
+        compiler_params=pltpu.CompilerParams(
+            vmem_limit_bytes=60 << 20, collective_id=0, has_side_effects=True
+        ),
         name="attention",
     )(
-        hidden[0], queries[0], cosine, sine, pages, fresh, krel, kv_up, out_proj,
+        hidden[0], queries[0], cosine, sine, own, old_rel, kv_up, out_proj,
         norm_gain[None], routes[0].T,
     )
     sent = packed.reshape(devices, SLOTS, width)

time: 405 us -> 314 us (0.78)
  waiting for transfers between devices: 184 us -> 98.4 us
  between operations: 14.8 us -> 1.39 us
  Pallas kernels: 74.8 us -> 85.5 us
    all_gather x2 -> x0, waiting for transfers between devices: 84.6 us -> none  [the longest x1 44.5 us: local(): fresh = lax.all_gather(new_latent[None], 'tok', axis=0, tiled=True)]
    pallas_call x1, Pallas kernels: 40.9 us -> 51.6 us  [local(): pl.pallas_call(attention_kernel, out_shape=(jax.ShapeDtypeStruct((rows, w...]
    all_gather x1 -> x0, local copies, waits for them, and re-layouts: 4.38 us -> none  [local(): pages = lax.all_gather(latent_cache[0], 'tok', axis=0, tiled=True)]
  transfers between devices with their start and end apart: 3 -> 1, of which waited for: 3 -> 1; matrix products, arithmetic and copies ran while one was open for 3% -> 1% of each run, Pallas kernels for 0% -> 0%
where the time goes in v2:
time: 314 us; the launch traced here: 308 us
  blocking collectives  105 us (33%)
  waiting for transfers between devices  98.4 us (31%)
  Pallas kernels  85.5 us (27%)
  starting transfers between devices  7.69 us (2%)
  local copies, waits for them, and re-layouts  6.49 us (2%)
  other arithmetic  3.48 us (1%)
    all_to_all x1, blocking collectives, local(): lax.all_to_all(sent, ('req', 'tok'), split_axis=0, concat_axis=0, tiled=T...  105 us
    all_to_all x1, waiting for transfers between devices, local(): lax.all_to_all(results, ('req', 'tok'), split_axis=0, concat_axis=0, tile...  98.4 us
    pallas_call x1, Pallas kernels, local(): pl.pallas_call(attention_kernel, out_shape=(jax.ShapeDtypeStruct((rows, w...  51.6 us
    pallas_call x1, Pallas kernels, local(): pl.pallas_call(expert_kernel, out_shape=jax.ShapeDtypeStruct((devices, SL...  25.8 us
    pallas_call x1, Pallas kernels, local(): pl.pallas_call(combine_kernel, out_shape=jax.ShapeDtypeStruct((rows, widt...  8.05 us
    all_to_all x1, starting transfers between devices, local(): lax.all_to_all(results, ('req', 'tok'), split_axis=0, concat_axis=0, tile...  7.69 us
  transfers between devices with their start and end apart: 1, of which 1 were waited for; matrix products, arithmetic and copies ran while one was open for 1% of the time, Pallas kernels for 0%

profile of v2, /device:TPU:31, one launch (start us, length us, event | category | flops | bytes accessed | tf_op | source)
XLA Modules:
  0.0 308.2 jit_solution(16216415427824966626)
XLA Ops:
  0.6 1.1 copy.29
  1.7 1.1 copy.30
  3.5 0.1 multiply_reduce_fusion
  3.6 0.8 select_reduce_fusion
  4.4 1.3 copy.37
  5.7 0.3 fusion.2
  6.0 0.8 multiply_convert_fusion
  6.8 0.7 compare_select_fusion.old_rel
  7.5 0.8 fusion.1
  8.2 0.8 concatenate.18.own
  9.0 51.6 %attention.1 = (f32[128,2048]{1,0:T(8,128)}, bf16[64,2,16,2048]{3,2,1,0:T(8,128)(2,1)}) custom-call(bf16[128,2048]{1,0:T(8,128)(2,1)} %bitcast.30, bf16[128,3072]{1,0:T(8,128)(2,1)} %bitcast.27, f32[128,64]{1,0:T(8,128)} %get-tuple-element.16.cosine, f32[128,64]{1,0:T(8,128)} %get-tuple-element.13.sine, bf16[128,1152]{1,0:T(8,128)(2,1)} %concatenate.18.own, ...), custom_call_target="tpu_custom_call" | custom-call | tf_op jit(solution)/shard_map/attention/pallas_call | solution.py:365
  60.6 105.3 %all_to_all.10.rows_ref = bf16[128,16,2048]{2,1,0:T(8,128)(2,1)} all-to-all(bf16[128,16,2048]{2,1,0:T(8,128)(2,1)} %bitcast.24), channel_id=1, replica_groups=mesh['req'=8,'tok'=16] {'req','tok'}, dimensions={0} | all-to-all | bytes 16777216 | tf_op jit(solution)/shard_map/all_to_all | solution.py:399
  165.9 25.8 %experts.1 = bf16[128,16,2048]{2,1,0:T(8,128)(2,1)} custom-call(bf16[128,16,2048]{2,1,0:T(8,128)(2,1)} %all_to_all.10.rows_ref, bf16[2048,1408]{1,0:T(8,128)(2,1)} %bitcast.25, bf16[704,2048]{1,0:T(8,128)(2,1)} %bitcast.26), custom_call_target="tpu_custom_call" | custom-call | tf_op jit(solution)/shard_map/experts/pallas_call | solution.py:402
  191.8 0.0 copy-start
  191.8 0.0 copy-start.1
  191.8 7.7 %all-to-all-start.1 = ((bf16[128,16,2048]{2,1,0:T(8,128)(2,1)}), bf16[128,16,2048]{2,1,0:T(8,128)(2,1)}, u32[]{:S(2)}, u32[]{:S(2)}) async-start(bf16[128,16,2048]{2,1,0:T(8,128)(2,1)} %experts.1), calls=%async_computation.1 | async-start | bytes 16777216 | tf_op jit(solution)/shard_map/all_to_all | solution.py:415
  199.5 0.0 copy-done
  199.5 0.7 copy.31
  200.2 0.0 copy-done.1
  200.2 0.7 copy.33
  201.0 0.8 copy.34
  201.7 98.4 %all-to-all-done.1 = bf16[128,16,2048]{2,1,0:T(8,128)(2,1)} async-done(((bf16[128,16,2048]{2,1,0:T(8,128)(2,1)}), bf16[128,16,2048]{2,1,0:T(8,128)(2,1)}, u32[]{:S(2)}, u32[]{:S(2)}) %all-to-all-start.1) | async-done | bytes 8388640 | tf_op jit(solution)/shard_map/all_to_all | solution.py:415
  300.1 8.1 %combine.1 = bf16[128,2048]{1,0:T(8,128)(2,1)} custom-call(bf16[64,2,16,2048]{3,2,1,0:T(8,128)(2,1)} %bitcast.14.returned, f32[128,2048]{1,0:T(8,128)} %get-tuple-element.5.residual, s32[128,6]{1,0:T(8,128)} %bitcast.32, f32[128,6]{1,0:T(8,128)} %bitcast.33), custom_call_target="tpu_custom_call" | custom-call | tf_op jit(solution)/shard_map/combine/pallas_call | solution.py:417
  (8 shorter events, 0.1 us)
Async XLA Ops:
  191.8 7.7 %copy-start = (s32[1,128,6]{1,0,2:T(1,128)S(1)}, s32[1,128,6]{1,0,2:T(1,128)}, u32[]{:S(2)}) copy-start(s32[1,128,6]{1,0,2:T(1,128)} %param.20) | copy-start | bytes 9220
  191.8 8.4 %copy-start.1 = (f32[1,128,6]{1,0,2:T(1,128)S(1)}, f32[1,128,6]{1,0,2:T(1,128)}, u32[]{:S(2)}) copy-start(f32[1,128,6]{1,0,2:T(1,128)} %param.21) | copy-start | bytes 9220
  191.8 108.4 %all-to-all-start.1 = ((bf16[128,16,2048]{2,1,0:T(8,128)(2,1)}), bf16[128,16,2048]{2,1,0:T(8,128)(2,1)}, u32[]{:S(2)}, u32[]{:S(2)}) async-start(bf16[128,16,2048]{2,1,0:T(8,128)(2,1)} %experts.1), calls=%async_computation.1 | async-start | bytes 16777216 | tf_op jit(solution)/shard_map/all_to_all | solution.py:415
